TPU v7x, 32 devices: a whole 2x2x4 slice. The times are simulated.
32 devices in a mesh: lon: 8 (over y, x, core), lat: 4 (over z).
Axes of the slice: x: 2, y: 2, z: 4, core: 2. Of those that a mesh axis runs over, the one named last changes fastest.
Arguments:
- ensemble: float32 [8, 4, 80, 32, 256], P('lon', 'lat'), may hold values from -6 to 6
- obs_block: int32 [3, 128], replicated, may hold values from 0 to 31, as said below
- obs_column: int32 [3, 128], replicated, may hold values from 0 to 255
- obs_value: float32 [3, 128], replicated, may hold values from -8 to 8
- obs_error: float32 [3, 128], replicated, may hold values from 0.5 to 2
- loc_mask: int32 [8, 4, 3, 128, 256], P('lon', 'lat'), may hold values from 0 to 1, as said below
Outputs:
- analysis: float32 [8, 4, 80, 32, 256], P('lon', 'lat')
Inputs may be any that keep to these rules, and one draw needn't show every extreme that they name: `obs_block`: observations fall more often on blocks of low index. `loc_mask`: an observation may update only columns of its own block and of blocks at most two blocks away along longitude (cyclically) and latitude; all other blocks have zeros for it.
All inputs are finite; a program needn't handle non-finite values.
Results may differ from a plain program's by a relative error of at most 0.0001.
Values sent between devices are 32-bit elements; how exact they have to be, the bound alone decides.
No kernel may reach another device: no remote copies, remote signals or barrier semaphores. Data moves between devices by JAX's collectives and lax.ppermute only.
A program may use at most 64 MiB of HBM per device.

v0:
```python
import jax
import jax.numpy as jnp
from jax import lax
from jax.sharding import PartitionSpec as P


def solve_rows(whitened, innov_raw):
    count = whitened.shape[0]
    cmat = jnp.eye(count, dtype=jnp.float32) + jnp.dot(
        whitened, whitened.T, precision=lax.Precision.HIGHEST
    )
    chol = jnp.linalg.cholesky(cmat)
    gain_rows = jax.scipy.linalg.cho_solve((chol, True), whitened)
    innov = jax.scipy.linalg.cho_solve((chol, True), innov_raw)
    return (gain_rows, innov)


def body(ensemble, obs_block, obs_column, obs_value, obs_error, loc_mask):
    members = ensemble.shape[2]
    levels = ensemble.shape[3]
    columns = ensemble.shape[4]
    count = obs_block.shape[1]
    scale = 1.0 / jnp.sqrt(jnp.float32(members - 1))
    n_lat = lax.axis_size("lat")
    lat_here = lax.axis_index("lat")
    state = ensemble.reshape(members, levels * columns)
    col_ids = jnp.arange(columns, dtype=jnp.int32)
    for batch in range(obs_block.shape[0]):
        blocks = obs_block[batch]
        pick = obs_column[batch][:, None] == col_ids[None, :]
        surface = state[:, :columns]
        piece = lax.all_gather(surface[None], "lon", axis=0, tiled=True)
        width = piece.shape[0]
        ids = jnp.arange(width, dtype=jnp.int32) * n_lat + lat_here
        select = ((blocks[:, None] == ids[None, :])[:, :, None] & pick[:, None, :]).astype(
            jnp.float32
        )
        row_part = jnp.zeros((count, members), jnp.float32) + jnp.einsum(
            "pkc,kmc->pm", select, piece, precision=lax.Precision.HIGHEST
        )
        obs_ens = lax.psum(row_part, "lat")
        obs_mean = jnp.mean(obs_ens, axis=1)
        errors = obs_error[batch]
        whitened = (obs_ens - obs_mean[:, None]) * scale / errors[:, None]
        innov_raw = (obs_value[batch] - obs_mean) / errors
        gain_rows, innov = solve_rows(whitened, innov_raw)
        coef = jnp.concatenate([-0.5 * gain_rows.T, (innov * scale)[None, :]], axis=0)
        weights = loc_mask[0, 0, batch].astype(jnp.float32)
        mean = jnp.mean(state, axis=0)
        pert = state - mean[None, :]
        proj = jnp.dot(whitened, pert, precision=lax.Precision.HIGHEST)
        proj = (proj.reshape(count, levels, columns) * weights[:, None, :]).reshape(
            count, levels * columns
        )
        incr = jnp.dot(coef, proj, precision=lax.Precision.HIGHEST)
        state = pert + incr[:members] + (mean + incr[members])[None, :]
    return state.reshape(ensemble.shape)


def solution(mesh):
    placed = (
        P("lon", "lat", None, None, None),
        P(),
        P(),
        P(),
        P(),
        P("lon", "lat", None, None, None),
    )
    return jax.shard_map(
        body,
        mesh=mesh,
        in_specs=placed,
        out_specs=P("lon", "lat", None, None, None),
        check_vma=False,
    )
```

profile of v0, /device:TPU:0, one launch (start us, length us, event | category | flops | bytes accessed | tf_op | source)
XLA Modules:
  0.0 211.4 jit_solution(10639633567476785206)
XLA Ops:
  0.9 3.4 %copy.32 = f32[10,8,32,256]{3,1,2,0:T(8,128)S(1)} copy(f32[10,8,32,256]{3,2,1,0:T(8,128)} %bitcast.215) | data formatting | bytes 5242880
  4.3 11.6 %all-gather = f32[640,256]{1,0:T(8,128)S(1)} all-gather(f32[80,256]{1,0:T(8,128)S(1)} %slice.116), channel_id=2, replica_groups=mesh['lon'=8,'lat'=4] {'lon'}, dimensions={0}, use_global_device_ids=true | all-gather | bytes 737280 | tf_op jit(solution)/shard_map/all_gather | solution.py:32
  16.8 19.8 %psum.21 = f32[128,80]{0,1:T(8,128)S(1)} all-reduce(f32[128,80]{0,1:T(8,128)S(1)} %convolution_bitcast_fusion.2), channel_id=1, replica_groups=mesh['lon'=8,'lat'=4] {'lat'}, use_global_device_ids=true, to_apply=%region_1.0 | all-reduce | flops 10240 | bytes 81920 | tf_op jit(solution)/shard_map/psum | solution.py:41
  37.1 11.7 %cholesky.59 = f32[128,128]{1,0:T(8,128)S(1)} custom-call(f32[128,128]{1,0:T(8,128)S(1)} %fusion.63), custom_call_target="Cholesky" | custom-call | tf_op jit(solution)/shard_map/jit(cholesky)/cholesky | solution.py:12
  50.1 9.8 %custom-call.16 = f32[1,128,128]{1,2,0:T(8,128)S(1)} custom-call(f32[1,128,128]{2,1,0:T(8,128)S(1)} %fusion.31), custom_call_target="InvertDiagBlocksLowerTriangular" | custom-call | tf_op jit(solution)/shard_map/jit(_cho_solve)/triangular_solve | solution.py:13
  61.0 1.9 reduce_sum.54
  64.0 5.1 %fusion.8 = f32[128,32,256]{2,0,1:T(8,128)} fusion(f32[10,32,8,256]{3,2,1,0:T(8,128)S(1)} %bitcast.216, f32[128,256]{1,0:T(8,128)S(1)} %get-tuple-element.13, f32[128,80]{0,1:T(8,128)S(1)} %psum.21, f32[128]{0:T(128)S(1)} %get-tuple-element.18, f32[128]{0:T(128)S(1)} %broadcast_multiply_fusion.4), kind=kOutput, calls=%fused_computation.13 | convolution fusion | flops 1007712256 | bytes 6988800 | tf_op jit(solution)/shard_map/dot_general | solution.py:51
  69.1 5.6 %copy.21 = f32[128,32,256]{0,2,1:T(8,128)} copy(f32[128,32,256]{2,0,1:T(8,128)} %fusion.8) | data formatting | bytes 8388608 | tf_op jit(solution)/shard_map/mul | solution.py:52
  74.7 5.9 %fusion.34 = f32[81,8192]{1,0:T(8,128)S(1)} fusion(f32[128,8192]{0,1:T(8,128)} %bitcast.210, f32[1,128]{0,1:T(8,128)S(1)} %copy.19, f32[80,128]{0,1:T(8,128)S(1)} %fusion.15), kind=kOutput, calls=%fused_computation.62 | convolution fusion | flops 1019226240 | bytes 6889984 | tf_op jit(solution)/shard_map/dot_general | solution.py:55
  82.6 10.1 %all-gather.1 = f32[640,256]{1,0:T(8,128)S(1)} all-gather(f32[80,256]{1,0:T(8,128)S(1)} %slice.119), channel_id=3, replica_groups=mesh['lon'=8,'lat'=4] {'lon'}, dimensions={0}, use_global_device_ids=true | all-gather | bytes 737280 | tf_op jit(solution)/shard_map/all_gather | solution.py:32
  93.6 16.3 %psum.22 = f32[128,80]{0,1:T(8,128)S(1)} all-reduce(f32[128,80]{0,1:T(8,128)S(1)} %convolution_bitcast_fusion.1), channel_id=1, replica_groups=mesh['lon'=8,'lat'=4] {'lat'}, use_global_device_ids=true, to_apply=%region_6.0 | all-reduce | flops 10240 | bytes 81920 | tf_op jit(solution)/shard_map/psum | solution.py:41
  110.3 11.7 %cholesky.70 = f32[128,128]{1,0:T(8,128)S(1)} custom-call(f32[128,128]{1,0:T(8,128)S(1)} %fusion.57), custom_call_target="Cholesky" | custom-call | tf_op jit(solution)/shard_map/jit(cholesky)/cholesky | solution.py:12
  123.5 9.8 %custom-call.18 = f32[1,128,128]{1,2,0:T(8,128)S(1)} custom-call(f32[1,128,128]{2,1,0:T(8,128)S(1)} %fusion.32), custom_call_target="InvertDiagBlocksLowerTriangular" | custom-call | tf_op jit(solution)/shard_map/jit(_cho_solve)/triangular_solve | solution.py:13
  134.7 3.3 %copy.35 = f32[16,8,32,256]{3,1,2,0:T(8,128)S(1)} copy(f32[16,8,32,256]{3,2,1,0:T(8,128)S(1)} %bitcast.213) | data formatting | bytes 8388608
  138.1 4.0 %convolution_multiply_fusion.1 = f32[128,8192]{1,0:T(8,128)S(1)} fusion(f32[128,8192]{1,0:T(8,128)S(1)} %bitcast.211, f32[80,8192]{1,0:T(8,128)S(1)} %copy-done.1, f32[8192]{0:T(1024)S(1)} %broadcast_multiply_fusion.1, f32[128,80]{0,1:T(8,128)S(1)} %psum.22, f32[128]{0:T(128)S(1)} %get-tuple-element.19, f32[128]{0:T(128)S(1)} %broadcast_multiply_fusion.3), kind=kOutput, calls=%fused_computation.1 | convolution fusion | flops 1008367616 | bytes 11084800 | tf_op jit(solution)/shard_map/dot_general | solution.py:51
  142.0 3.0 %fusion.38 = f32[81,8192]{1,0:T(8,128)S(1)} fusion(f32[128,8192]{1,0:T(8,128)S(1)} %convolution_multiply_fusion.1, f32[1,128]{0,1:T(8,128)S(1)} %copy.24, f32[80,128]{0,1:T(8,128)S(1)} %fusion.14), kind=kOutput, calls=%fused_computation.66 | convolution fusion | flops 1019226240 | bytes 6889984 | tf_op jit(solution)/shard_map/dot_general | solution.py:55
  145.6 9.2 %all-gather.2 = f32[640,256]{1,0:T(8,128)S(1)} all-gather(f32[80,256]{1,0:T(8,128)S(1)} %slice.122), channel_id=4, replica_groups=mesh['lon'=8,'lat'=4] {'lon'}, dimensions={0}, use_global_device_ids=true | all-gather | bytes 737280 | tf_op jit(solution)/shard_map/all_gather | solution.py:32
  155.6 18.1 %psum.23 = f32[128,80]{0,1:T(8,128)S(1)} all-reduce(f32[128,80]{0,1:T(8,128)S(1)} %convolution_bitcast_fusion), channel_id=1, replica_groups=mesh['lon'=8,'lat'=4] {'lat'}, use_global_device_ids=true, to_apply=%region_9.13 | all-reduce | flops 10240 | bytes 81920 | tf_op jit(solution)/shard_map/psum | solution.py:41
  174.2 11.7 %cholesky.81 = f32[128,128]{1,0:T(8,128)S(1)} custom-call(f32[128,128]{1,0:T(8,128)S(1)} %fusion.51), custom_call_target="Cholesky" | custom-call | tf_op jit(solution)/shard_map/jit(cholesky)/cholesky | solution.py:12
  187.2 9.8 %custom-call.20 = f32[1,128,128]{1,2,0:T(8,128)S(1)} custom-call(f32[1,128,128]{2,1,0:T(8,128)S(1)} %fusion.33), custom_call_target="InvertDiagBlocksLowerTriangular" | custom-call | tf_op jit(solution)/shard_map/jit(_cho_solve)/triangular_solve | solution.py:13
  198.4 3.3 %copy.36 = f32[16,8,32,256]{3,1,2,0:T(8,128)S(1)} copy(f32[16,8,32,256]{3,2,1,0:T(8,128)S(1)} %bitcast.214) | data formatting | bytes 8388608
  201.7 3.8 %convolution_multiply_fusion = f32[128,8192]{1,0:T(8,128)S(1)} fusion(f32[128,8192]{1,0:T(8,128)S(1)} %bitcast.212, f32[80,8192]{1,0:T(8,128)S(1)} %get-tuple-element.8, f32[8192]{0:T(1024)S(1)} %broadcast_multiply_fusion, f32[128,80]{0,1:T(8,128)S(1)} %psum.23, f32[128]{0:T(128)S(1)} %get-tuple-element.17, f32[128]{0:T(128)S(1)} %broadcast_multiply_fusion.2), kind=kOutput, calls=%fused_computation | convolution fusion | flops 1008367616 | bytes 11084800 | tf_op jit(solution)/shard_map/dot_general | solution.py:51
  205.5 3.0 %fusion.42 = f32[81,8192]{1,0:T(8,128)S(1)} fusion(f32[128,8192]{1,0:T(8,128)S(1)} %convolution_multiply_fusion, f32[1,128]{0,1:T(8,128)S(1)} %copy.27, f32[80,128]{0,1:T(8,128)S(1)} %fusion.13), kind=kOutput, calls=%fused_computation.70 | convolution fusion | flops 1019226240 | bytes 6889984 | tf_op jit(solution)/shard_map/dot_general | solution.py:55
  208.9 2.3 %copy.37 = f32[10,8,32,256]{3,2,1,0:T(8,128)} copy(f32[10,8,32,256]{3,1,2,0:T(8,128)S(1)} %bitcast.217) | data formatting | bytes 5242880
  (80 shorter events, 16.4 us)
Async XLA Ops:
  0.9 15.1 %copy-start.5 = (s32[3,128]{1,0:T(4,128)S(1)}, s32[3,128]{1,0:T(4,128)}, u32[]{:S(2)}) copy-start(s32[3,128]{1,0:T(4,128)} %param.13) | copy-start | bytes 4612
  0.9 35.8 %copy-start.3 = (f32[3,128]{1,0:T(4,128)S(1)}, f32[3,128]{1,0:T(4,128)}, u32[]{:S(2)}) copy-start(f32[3,128]{1,0:T(4,128)} %param.15) | copy-start | bytes 4612
  4.3 56.2 %copy-start.4 = (f32[3,128]{1,0:T(4,128)S(1)}, f32[3,128]{1,0:T(4,128)}, u32[]{:S(2)}) copy-start(f32[3,128]{1,0:T(4,128)} %param.14) | copy-start | bytes 4612
  62.9 1.0 copy-start.2
  81.1 1.5 copy-start
  134.7 3.4 %copy-start.1 = (f32[80,8192]{1,0:T(8,128)S(1)}, f32[80,8192]{1,0:T(8,128)}, u32[]{:S(2)}) copy-start(f32[80,8192]{1,0:T(8,128)} %copy-done) | copy-start | bytes 7864324
where the time goes:
time: 215 us; the launch traced here: 211 us
  blocking collectives  85.1 us (40%)
  other arithmetic  72.7 us (34%)
  matrix products  30.5 us (14%)
  local copies, waits for them, and re-layouts  22.4 us (10%)
    psum x3, blocking collectives, body(): obs_ens = lax.psum(row_part, 'lat')  54.3 us
    another operation x9, other arithmetic, solve_rows(): chol = jnp.linalg.cholesky(cmat)  37.2 us
    another operation x6, other arithmetic, solve_rows(): gain_rows = jax.scipy.linalg.cho_solve((chol, True), whitened)  31.4 us
    all_gather x3, blocking collectives, body(): piece = lax.all_gather(surface[None], 'lon', axis=0, tiled=True)  30.9 us
    unnamed x18, local copies, waits for them, and re-layouts  14.6 us
    dot_general x3, matrix products, body(): proj = jnp.dot(whitened, pert, precision=lax.Precision.HIGHEST)  12.9 us
    dot_general x3, matrix products, body(): incr = jnp.dot(coef, proj, precision=lax.Precision.HIGHEST)  12 us
    mul x3, local copies, waits for them, and re-layouts, body(): proj.reshape(count, levels, columns) * weights[:, None, :]  6.22 us

commit v1 on v0

--- a/solution.py
+++ b/solution.py
@@ -2,6 +2,18 @@
 import jax.numpy as jnp
 from jax import lax
 from jax.sharding import PartitionSpec as P
+
+
+def doubled_up(x, axis, dim):
+    ways, here = (lax.axis_size(axis), lax.axis_index(axis))
+    grown, reach = (x, 1)
+    while reach < ways:
+        theirs = lax.ppermute(grown, axis, [(d, d ^ reach) for d in range(ways)])
+        mine_first = jnp.concatenate([grown, theirs], axis=dim)
+        theirs_first = jnp.concatenate([theirs, grown], axis=dim)
+        grown = jnp.where(here & reach == 0, mine_first, theirs_first)
+        reach = 2 * reach
+    return grown
 
 
 def solve_rows(whitened, innov_raw):
@@ -29,7 +41,7 @@
         blocks = obs_block[batch]
         pick = obs_column[batch][:, None] == col_ids[None, :]
         surface = state[:, :columns]
-        piece = lax.all_gather(surface[None], "lon", axis=0, tiled=True)
+        piece = doubled_up(surface[None], "lon", 0)
         width = piece.shape[0]
         ids = jnp.arange(width, dtype=jnp.int32) * n_lat + lat_here
         select = ((blocks[:, None] == ids[None, :])[:, :, None] & pick[:, None, :]).astype(

time: 215 us -> 237 us (1.10)
  blocking collectives: 85.1 us -> 55 us
  waiting for transfers between devices: 0 us -> 26.5 us
  starting transfers between devices: 0 us -> 11.3 us
  matrix products: 30.5 us -> 39.1 us
  other arithmetic: 72.7 us -> 76.3 us
  local copies, waits for them, and re-layouts: 22.4 us -> 25 us
    all_gather x3 -> x0, blocking collectives: 30.9 us -> none  [body(): piece = lax.all_gather(surface[None], 'lon', axis=0, tiled=True)]
    ppermute x0 -> x9, waiting for transfers between devices: none -> 26.5 us  [doubled_up(): theirs = lax.ppermute(grown, axis, [(d, d ^ reach) for d in range(ways)])]
    ppermute x0 -> x9, starting transfers between devices: none -> 11.3 us  [doubled_up(): theirs = lax.ppermute(grown, axis, [(d, d ^ reach) for d in range(ways)])]
    dot_general x3, matrix products: 12.9 us -> 18.5 us  [body(): proj = jnp.dot(whitened, pert, precision=lax.Precision.HIGHEST)]
    unnamed x18 -> x38, local copies, waits for them, and re-layouts: 14.6 us -> 16.9 us
  transfers between devices with their start and end apart: 0 -> 9, of which waited for: 0 -> 8; matrix products, arithmetic and copies ran while one was open for 0% -> 8% of each run, Pallas kernels for 0% -> 0%
where the time goes in v1:
time: 237 us; the launch traced here: 234 us
  other arithmetic  76.3 us (32%)
  blocking collectives  55 us (23%)
  matrix products  39.1 us (16%)
  waiting for transfers between devices  26.5 us (11%)
  local copies, waits for them, and re-layouts  25 us (11%)
  starting transfers between devices  11.3 us (5%)
    psum x3, blocking collectives, body(): obs_ens = lax.psum(row_part, 'lat')  55 us
    another operation x9, other arithmetic, solve_rows(): chol = jnp.linalg.cholesky(cmat)  37.3 us
    another operation x6, other arithmetic, solve_rows(): gain_rows = jax.scipy.linalg.cho_solve((chol, True), whitened)  31.4 us
    ppermute x9, waiting for transfers between devices, doubled_up(): theirs = lax.ppermute(grown, axis, [(d, d ^ reach) for d in range(ways)])  26.5 us
    dot_general x3, matrix products, body(): proj = jnp.dot(whitened, pert, precision=lax.Precision.HIGHEST)  18.5 us
    unnamed x38, local copies, waits for them, and re-layouts  16.9 us
    dot_general x3, matrix products, body(): incr = jnp.dot(coef, proj, precision=lax.Precision.HIGHEST)  12.3 us
    ppermute x9, starting transfers between devices, doubled_up(): theirs = lax.ppermute(grown, axis, [(d, d ^ reach) for d in range(ways)])  11.3 us
  transfers between devices with their start and end apart: 9, of which 8 were waited for; matrix products, arithmetic and copies ran while one was open for 8% of the time, Pallas kernels for 0%

profile of v1, /device:TPU:0, one launch (start us, length us, event | category | flops | bytes accessed | tf_op | source)
XLA Modules:
  0.0 233.9 jit_solution(14131003846801823058)
XLA Ops:
  0.0 3.4 %copy.32 = f32[10,8,32,256]{3,1,2,0:T(8,128)S(1)} copy(f32[10,8,32,256]{3,2,1,0:T(8,128)} %bitcast.215) | data formatting | bytes 5242880
  9.0 2.6 %collective-permute-start.1 = (f32[2,80,256]{2,1,0:T(8,128)S(1)}, f32[2,80,256]{2,1,0:T(8,128)S(1)}, u32[]{:S(2)}, u32[]{:S(2)}) collective-permute-start(f32[2,80,256]{2,1,0:T(8,128)S(1)} %maximum_select_fusion.9), channel_id=1, source_target_pairs={{0,8},{4,12},{8,0},{12,4},{16,24},{20,28},{24,16},{28,20},{1,9},{5... | collective-permute-start | bytes 491528 | tf_op jit(solution)/shard_map/ppermute | solution.py:11
  12.2 4.2 %collective-permute-done.1 = f32[2,80,256]{2,1,0:T(8,128)S(1)} collective-permute-done((f32[2,80,256]{2,1,0:T(8,128)S(1)}, f32[2,80,256]{2,1,0:T(8,128)S(1)}, u32[]{:S(2)}, u32[]{:S(2)}) %collective-permute-start.1) | collective-permute-done | bytes 163872 | tf_op jit(solution)/shard_map/ppermute | solution.py:11
  20.2 6.8 %collective-permute-done.2 = f32[4,80,256]{2,1,0:T(8,128)} collective-permute-done((f32[4,80,256]{2,1,0:T(8,128)}, f32[4,80,256]{2,1,0:T(8,128)}, u32[]{:S(2)}, u32[]{:S(2)}) %collective-permute-start.2) | collective-permute-done | bytes 327712 | tf_op jit(solution)/shard_map/ppermute | solution.py:11
  29.0 20.2 %psum.21 = f32[128,80]{0,1:T(8,128)S(1)} all-reduce(f32[128,80]{0,1:T(8,128)S(1)} %convolution_bitcast_fusion.2), channel_id=1, replica_groups=mesh['lon'=8,'lat'=4] {'lat'}, use_global_device_ids=true, to_apply=%region_1.2 | all-reduce | flops 10240 | bytes 81920 | tf_op jit(solution)/shard_map/psum | solution.py:53
  50.4 11.7 %cholesky.59 = f32[128,128]{1,0:T(8,128)S(1)} custom-call(f32[128,128]{1,0:T(8,128)S(1)} %fusion.81), custom_call_target="Cholesky" | custom-call | tf_op jit(solution)/shard_map/jit(cholesky)/cholesky | solution.py:24
  63.6 9.8 %custom-call.16 = f32[1,128,128]{1,2,0:T(8,128)S(1)} custom-call(f32[1,128,128]{2,1,0:T(8,128)S(1)} %fusion.49), custom_call_target="InvertDiagBlocksLowerTriangular" | custom-call | tf_op jit(solution)/shard_map/jit(_cho_solve)/triangular_solve | solution.py:25
  75.0 7.3 %fusion.8 = f32[128,32,256]{2,0,1:T(8,128)} fusion(f32[10,32,8,256]{3,2,1,0:T(8,128)} %bitcast.216, f32[128,256]{1,0:T(8,128)S(1)} %get-tuple-element.13, f32[128,80]{0,1:T(8,128)S(1)} %psum.21, f32[128]{0:T(128)S(1)} %copy-done.9, f32[128]{0:T(128)S(1)} %broadcast_multiply_fusion.4), kind=kOutput, calls=%fused_computation.13 | convolution fusion | flops 1007712256 | bytes 6988800 | tf_op jit(solution)/shard_map/dot_general | solution.py:63
  82.3 5.6 %copy.21 = f32[128,32,256]{0,2,1:T(8,128)} copy(f32[128,32,256]{2,0,1:T(8,128)} %fusion.8) | data formatting | bytes 8388608 | tf_op jit(solution)/shard_map/mul | solution.py:64
  87.9 6.1 %fusion.52 = f32[81,8192]{1,0:T(8,128)S(1)} fusion(f32[128,8192]{0,1:T(8,128)} %bitcast.210, f32[1,128]{0,1:T(8,128)S(1)} %copy.19, f32[80,128]{0,1:T(8,128)S(1)} %fusion.15), kind=kOutput, calls=%fused_computation.92 | convolution fusion | flops 1019226240 | bytes 6889984 | tf_op jit(solution)/shard_map/dot_general | solution.py:67
  97.4 4.8 %collective-permute-done.4 = f32[2,80,256]{2,1,0:T(8,128)S(1)} collective-permute-done((f32[2,80,256]{2,1,0:T(8,128)S(1)}, f32[2,80,256]{2,1,0:T(8,128)S(1)}, u32[]{:S(2)}, u32[]{:S(2)}) %collective-permute-start.4) | collective-permute-done | bytes 163872 | tf_op jit(solution)/shard_map/ppermute | solution.py:11
  104.3 5.2 %copy.35 = f32[16,8,32,256]{3,1,2,0:T(8,128)} copy(f32[16,8,32,256]{3,2,1,0:T(8,128)S(1)} %bitcast.213) | data formatting | bytes 8388608
  112.0 16.3 %psum.22 = f32[128,80]{0,1:T(8,128)S(1)} all-reduce(f32[128,80]{0,1:T(8,128)S(1)} %convolution_bitcast_fusion.1), channel_id=1, replica_groups=mesh['lon'=8,'lat'=4] {'lat'}, use_global_device_ids=true, to_apply=%region_6.10 | all-reduce | flops 10240 | bytes 81920 | tf_op jit(solution)/shard_map/psum | solution.py:53
  128.7 11.7 %cholesky.70 = f32[128,128]{1,0:T(8,128)S(1)} custom-call(f32[128,128]{1,0:T(8,128)S(1)} %fusion.75), custom_call_target="Cholesky" | custom-call | tf_op jit(solution)/shard_map/jit(cholesky)/cholesky | solution.py:24
  141.8 9.8 %custom-call.18 = f32[1,128,128]{1,2,0:T(8,128)S(1)} custom-call(f32[1,128,128]{2,1,0:T(8,128)S(1)} %fusion.50), custom_call_target="InvertDiagBlocksLowerTriangular" | custom-call | tf_op jit(solution)/shard_map/jit(_cho_solve)/triangular_solve | solution.py:25
  152.6 5.6 %convolution_multiply_fusion.1 = f32[128,8192]{1,0:T(8,128)S(1)} fusion(f32[128,8192]{1,0:T(8,128)} %bitcast.212, f32[80,8192]{1,0:T(8,128)S(1)} %copy-done.1, f32[8192]{0:T(1024)S(1)} %broadcast_multiply_fusion.1, f32[128,80]{0,1:T(8,128)S(1)} %psum.22, f32[128]{0:T(128)S(1)} %copy-done.8, f32[128]{0:T(128)S(1)} %broadcast_multiply_fusion.3), kind=kOutput, calls=%fused_computation.1 | convolution fusion | flops 1008367616 | bytes 11084800 | tf_op jit(solution)/shard_map/dot_general | solution.py:63
  158.2 3.0 %fusion.56 = f32[81,8192]{1,0:T(8,128)S(1)} fusion(f32[128,8192]{1,0:T(8,128)S(1)} %convolution_multiply_fusion.1, f32[1,128]{0,1:T(8,128)S(1)} %copy.24, f32[80,128]{0,1:T(8,128)S(1)} %fusion.14), kind=kOutput, calls=%fused_computation.96 | convolution fusion | flops 1019226240 | bytes 6889984 | tf_op jit(solution)/shard_map/dot_general | solution.py:67
  164.7 4.8 %collective-permute-done.7 = f32[2,80,256]{2,1,0:T(8,128)S(1)} collective-permute-done((f32[2,80,256]{2,1,0:T(8,128)S(1)}, f32[2,80,256]{2,1,0:T(8,128)S(1)}, u32[]{:S(2)}, u32[]{:S(2)}) %collective-permute-start.7) | collective-permute-done | bytes 163872 | tf_op jit(solution)/shard_map/ppermute | solution.py:11
  171.6 5.2 %copy.36 = f32[16,8,32,256]{3,1,2,0:T(8,128)} copy(f32[16,8,32,256]{3,2,1,0:T(8,128)S(1)} %bitcast.214) | data formatting | bytes 8388608
  179.3 18.4 %psum.23 = f32[128,80]{0,1:T(8,128)S(1)} all-reduce(f32[128,80]{0,1:T(8,128)S(1)} %convolution_bitcast_fusion), channel_id=1, replica_groups=mesh['lon'=8,'lat'=4] {'lat'}, use_global_device_ids=true, to_apply=%region_9.13 | all-reduce | flops 10240 | bytes 81920 | tf_op jit(solution)/shard_map/psum | solution.py:53
  198.2 11.7 %cholesky.81 = f32[128,128]{1,0:T(8,128)S(1)} custom-call(f32[128,128]{1,0:T(8,128)S(1)} %fusion.69), custom_call_target="Cholesky" | custom-call | tf_op jit(solution)/shard_map/jit(cholesky)/cholesky | solution.py:24
  211.3 9.8 %custom-call.20 = f32[1,128,128]{1,2,0:T(8,128)S(1)} custom-call(f32[1,128,128]{2,1,0:T(8,128)S(1)} %fusion.51), custom_call_target="InvertDiagBlocksLowerTriangular" | custom-call | tf_op jit(solution)/shard_map/jit(_cho_solve)/triangular_solve | solution.py:25
  222.1 5.6 %convolution_multiply_fusion = f32[128,8192]{1,0:T(8,128)S(1)} fusion(f32[128,8192]{1,0:T(8,128)} %bitcast.211, f32[80,8192]{1,0:T(8,128)S(1)} %get-tuple-element.8, f32[8192]{0:T(1024)S(1)} %broadcast_multiply_fusion, f32[128,80]{0,1:T(8,128)S(1)} %psum.23, f32[128]{0:T(128)S(1)} %copy-done.7, f32[128]{0:T(128)S(1)} %broadcast_multiply_fusion.2), kind=kOutput, calls=%fused_computation | convolution fusion | flops 1008367616 | bytes 11084800 | tf_op jit(solution)/shard_map/dot_general | solution.py:63
  227.7 3.2 %fusion.60 = f32[81,8192]{1,0:T(8,128)S(1)} fusion(f32[128,8192]{1,0:T(8,128)S(1)} %convolution_multiply_fusion, f32[1,128]{0,1:T(8,128)S(1)} %copy.27, f32[80,128]{0,1:T(8,128)S(1)} %fusion.13), kind=kOutput, calls=%fused_computation.100 | convolution fusion | flops 1019226240 | bytes 6889984 | tf_op jit(solution)/shard_map/dot_general | solution.py:67
  (121 shorter events, 40.3 us)
Async XLA Ops:
  0.0 4.0 %copy-start.12 = (s32[3,128]{1,0:T(4,128)S(1)}, s32[3,128]{1,0:T(4,128)}, u32[]{:S(2)}) copy-start(s32[3,128]{1,0:T(4,128)} %param.12) | copy-start | bytes 4612
  0.0 4.0 %copy-start.13 = (s32[3,128]{1,0:T(4,128)S(1)}, s32[3,128]{1,0:T(4,128)}, u32[]{:S(2)}) copy-start(s32[3,128]{1,0:T(4,128)} %param.13) | copy-start | bytes 4612
  3.4 5.5 %collective-permute-start = (f32[1,80,256]{2,1,0:T(8,128)S(1)}, f32[1,80,256]{2,1,0:T(8,128)S(1)}, u32[]{:S(2)}, u32[]{:S(2)}) collective-permute-start(f32[1,80,256]{2,1,0:T(8,128)S(1)} %slice_bitcast_fusion.2), channel_id=1, source_target_pairs={{0,4},{4,0},{8,12},{12,8},{16,20},{20,16},{24,28},{28,24},{1,5},{5... | collective-permute-start | bytes 245768 | tf_op jit(solution)/shard_map/ppermute | solution.py:11
  7.2 11.7 %copy-start.5 = (f32[3,128]{1,0:T(4,128)S(1)}, f32[3,128]{1,0:T(4,128)}, u32[]{:S(2)}) copy-start(f32[3,128]{1,0:T(4,128)} %param.15) | copy-start | bytes 4612
  7.2 12.9 %copy-start.3 = (s32[1,1,3,128,256]{4,3,2,1,0:T(8,128)S(1)}, s32[1,1,3,128,256]{4,3,2,1,0:T(8,128)}, u32[]{:S(2)}) copy-start(s32[1,1,3,128,256]{4,3,2,1,0:T(8,128)} %param.16) | copy-start | bytes 1179652
  9.0 65.5 %copy-start.6 = (f32[3,128]{1,0:T(4,128)S(1)}, f32[3,128]{1,0:T(4,128)}, u32[]{:S(2)}) copy-start(f32[3,128]{1,0:T(4,128)} %param.14) | copy-start | bytes 4612
  9.0 7.4 %collective-permute-start.1 = (f32[2,80,256]{2,1,0:T(8,128)S(1)}, f32[2,80,256]{2,1,0:T(8,128)S(1)}, u32[]{:S(2)}, u32[]{:S(2)}) collective-permute-start(f32[2,80,256]{2,1,0:T(8,128)S(1)} %maximum_select_fusion.9), channel_id=1, source_target_pairs={{0,8},{4,12},{8,0},{12,4},{16,24},{20,28},{24,16},{28,20},{1,9},{5... | collective-permute-start | bytes 491528 | tf_op jit(solution)/shard_map/ppermute | solution.py:11
  17.1 9.8 %collective-permute-start.2 = (f32[4,80,256]{2,1,0:T(8,128)}, f32[4,80,256]{2,1,0:T(8,128)}, u32[]{:S(2)}, u32[]{:S(2)}) collective-permute-start(f32[4,80,256]{2,1,0:T(8,128)} %maximum_select_fusion.6), channel_id=1, source_target_pairs={{0,16},{4,20},{8,24},{12,28},{16,0},{20,4},{24,8},{28,12},{1,17},{... | collective-permute-start | bytes 983048 | tf_op jit(solution)/shard_map/ppermute | solution.py:11
  20.2 54.9 %copy-start.9 = (f32[128]{0:T(128)S(1)}, f32[128]{0:T(128)}, u32[]{:S(2)}) copy-start(f32[128]{0:T(128)} %get-tuple-element.18) | copy-start | bytes 1540
  87.9 6.1 %copy-start.4 = (f32[1,1,32,256]{3,1,2,0:T(1,128)S(1)}, f32[1,1,32,256]{3,1,2,0:T(1,128)}, u32[]{:S(2)}) copy-start(f32[1,1,32,256]{3,1,2,0:T(1,128)} %copy.34) | copy-start | bytes 98308
  94.0 9.8 %copy-start.11 = (s32[128]{0:T(128)S(1)}, s32[128]{0:T(128)}, u32[]{:S(2)}) copy-start(s32[128]{0:T(128)} %get-tuple-element.25) | copy-start | bytes 1540
  94.5 9.8 %copy-start = (f32[80,8192]{1,0:T(8,128)}, f32[80,8192]{1,0:T(8,128)S(1)}, u32[]{:S(2)}) copy-start(f32[80,8192]{1,0:T(8,128)S(1)} %get-tuple-element.11) | copy-start | bytes 7864324
  94.5 1.3 collective-permute-start.3
  95.9 6.3 %collective-permute-start.4 = (f32[2,80,256]{2,1,0:T(8,128)S(1)}, f32[2,80,256]{2,1,0:T(8,128)S(1)}, u32[]{:S(2)}, u32[]{:S(2)}) collective-permute-start(f32[2,80,256]{2,1,0:T(8,128)S(1)} %maximum_select_fusion.10), channel_id=1, source_target_pairs={{0,8},{4,12},{8,0},{12,4},{16,24},{20,28},{24,16},{28,20},{1,9},{5... | collective-permute-start | bytes 491528 | tf_op jit(solution)/shard_map/ppermute | solution.py:11
  102.2 9.0 %collective-permute-start.5 = (f32[4,80,256]{2,1,0:T(8,128)S(1)}, f32[4,80,256]{2,1,0:T(8,128)S(1)}, u32[]{:S(2)}, u32[]{:S(2)}) collective-permute-start(f32[4,80,256]{2,1,0:T(8,128)S(1)} %maximum_select_fusion.7), channel_id=1, source_target_pairs={{0,16},{4,20},{8,24},{12,28},{16,0},{20,4},{24,8},{28,12},{1,17},{... | collective-permute-start | bytes 983048 | tf_op jit(solution)/shard_map/ppermute | solution.py:11
  104.2 7.0 %copy-start.15 = (pred[128,8]{0,1:T(8,128)(4,1)S(1)}, pred[128,8]{0,1:T(8,128)(4,1)}, u32[]{:S(2)}) copy-start(pred[128,8]{0,1:T(8,128)(4,1)} %get-tuple-element.27) | copy-start | bytes 3076
  104.3 24.1 %copy-start.8 = (f32[128]{0:T(128)S(1)}, f32[128]{0:T(128)}, u32[]{:S(2)}) copy-start(f32[128]{0:T(128)} %get-tuple-element.19) | copy-start | bytes 1540
  109.5 43.1 %copy-start.1 = (f32[80,8192]{1,0:T(8,128)S(1)}, f32[80,8192]{1,0:T(8,128)}, u32[]{:S(2)}) copy-start(f32[80,8192]{1,0:T(8,128)} %copy-done) | copy-start | bytes 7864324
  161.3 9.8 %copy-start.10 = (s32[128]{0:T(128)S(1)}, s32[128]{0:T(128)}, u32[]{:S(2)}) copy-start(s32[128]{0:T(128)} %get-tuple-element.23) | copy-start | bytes 1540
  161.8 1.3 collective-permute-start.6
  163.2 6.3 %collective-permute-start.7 = (f32[2,80,256]{2,1,0:T(8,128)S(1)}, f32[2,80,256]{2,1,0:T(8,128)S(1)}, u32[]{:S(2)}, u32[]{:S(2)}) collective-permute-start(f32[2,80,256]{2,1,0:T(8,128)S(1)} %maximum_select_fusion.11), channel_id=1, source_target_pairs={{0,8},{4,12},{8,0},{12,4},{16,24},{20,28},{24,16},{28,20},{1,9},{5... | collective-permute-start | bytes 491528 | tf_op jit(solution)/shard_map/ppermute | solution.py:11
  169.5 9.0 %collective-permute-start.8 = (f32[4,80,256]{2,1,0:T(8,128)S(1)}, f32[4,80,256]{2,1,0:T(8,128)S(1)}, u32[]{:S(2)}, u32[]{:S(2)}) collective-permute-start(f32[4,80,256]{2,1,0:T(8,128)S(1)} %maximum_select_fusion.8), channel_id=1, source_target_pairs={{0,16},{4,20},{8,24},{12,28},{16,0},{20,4},{24,8},{28,12},{1,17},{... | collective-permute-start | bytes 983048 | tf_op jit(solution)/shard_map/ppermute | solution.py:11
  171.6 7.0 %copy-start.14 = (pred[128,8]{0,1:T(8,128)(4,1)S(1)}, pred[128,8]{0,1:T(8,128)(4,1)}, u32[]{:S(2)}) copy-start(pred[128,8]{0,1:T(8,128)(4,1)} %get-tuple-element.26) | copy-start | bytes 3076
  171.6 26.2 %copy-start.7 = (f32[128]{0:T(128)S(1)}, f32[128]{0:T(128)}, u32[]{:S(2)}) copy-start(f32[128]{0:T(128)} %get-tuple-element.17) | copy-start | bytes 1540
  (1 other events, 3.1 us)
